TPU v7x, 256 devices: a whole 4x4x8 slice. The times are simulated.
256 devices in a mesh: section: 2 (over y_hi), seq: 32 (over x, z), chan: 4 (over y_lo, core).
Axes of the slice: x: 4, y: 4 (y_hi: 2, y_lo: 2; y = y_hi * 2 + y_lo), z: 8, core: 2. Of those that a mesh axis runs over, the one named last changes fastest.
Arguments:
- bases: int32 [2, 2097152], P('section', 'seq'), may hold values from 0 to 3
- stem_embedding_weight: bfloat16 [512, 1536], P(None, 'chan'), may hold values from -1.64443437 to 1.64443437
- gains: float32 [3, 1536], replicated, may hold values from 0.1 to 1.9
- conv_weight: bfloat16 [3, 3, 1536, 1536], P(None, None, None, 'chan'), may hold values from -0.09375 to 0.09375
- dec_weight: bfloat16 [1536, 384], P('chan'), may hold values from -0.3125 to 0.3125
- upstream: bfloat16 [2, 16384, 1536], P('section', 'seq', 'chan'), may hold values from -0.032958984 to 0.032958984
Outputs:
- decoded: bfloat16 [2, 16384, 1536], P('section', 'seq', 'chan')
- weight_grad: float32 [1536, 384], P('chan')
All inputs are finite; a program needn't handle non-finite values.
Results may differ from a plain program's by a relative error of at most 0.0076.
Values may be sent and summed in bfloat16 or wider, within the bound.
No kernel may reach another device: no remote copies, remote signals or barrier semaphores. Data moves between devices by JAX's collectives and lax.ppermute only.
A program may use at most 128 MiB of HBM per device.

v0:
```python
import jax
import jax.numpy as jnp
from jax import lax
from jax.sharding import PartitionSpec as P

PATCH = 128
FIRST_DILATION0 = 2
EPSILON = 1e-06


def with_halo(shard, sides, width):
    for axis, dim in sides:
        size, length = (lax.axis_size(axis), shard.shape[dim])
        up = [(i, (i + 1) % size) for i in range(size - 1)]
        down = [(j, i) for i, j in up]
        last = lax.slice_in_dim(shard, length - width, length, axis=dim)
        initial = lax.slice_in_dim(shard, 0, width, axis=dim)
        before = lax.ppermute(last, axis, up)
        after = lax.ppermute(initial, axis, down)
        shard = jnp.concatenate([before, shard, after], axis=dim)
    return shard


def activate(rows, gain_row):
    widened = rows.astype(jnp.float32)
    inverse_rms = lax.rsqrt(jnp.mean(widened * widened, axis=-1, keepdims=True) + EPSILON)
    return jax.nn.gelu(widened * inverse_rms * gain_row).astype(jnp.bfloat16)


def apply_convolution(padded, kernel_taps, dilation_step, row_count):
    update = jnp.dot(padded[0:row_count], kernel_taps[0], preferred_element_type=jnp.float32)
    for offset in range(1, kernel_taps.shape[0]):
        start = offset * dilation_step
        update = update + jnp.dot(
            padded[start : start + row_count],
            kernel_taps[offset],
            preferred_element_type=jnp.float32,
        )
    return update


def body(bases, stem_embedding_weight, gains, conv_weight, dec_weight, upstream):
    row_count = upstream.shape[1]
    letters = bases.reshape(row_count, PATCH)
    onehot = letters[:, :, None] == jnp.arange(4, dtype=jnp.int32)[None, None, :]
    onehot = onehot.astype(jnp.bfloat16).reshape(row_count, PATCH * 4)
    stream = jnp.dot(onehot, stem_embedding_weight, preferred_element_type=jnp.float32).astype(
        jnp.bfloat16
    )
    for tower_layer_index in range(conv_weight.shape[0]):
        dilation_step = FIRST_DILATION0 * 2**tower_layer_index
        full_rows = lax.all_gather(stream, "chan", axis=1, tiled=True)
        padded = with_halo(
            activate(full_rows, gains[tower_layer_index]), (("seq", 0),), dilation_step
        )
        update = apply_convolution(padded, conv_weight[tower_layer_index], dilation_step, row_count)
        stream = (stream.astype(jnp.float32) + update).astype(jnp.bfloat16)
    decoded = jnp.dot(stream, dec_weight, preferred_element_type=jnp.float32).astype(jnp.bfloat16)
    upstream_rows = upstream[0]
    contract_row_pairs = (((0,), (0,)), ((), ()))
    partial_grad = lax.dot_general(
        stream, upstream_rows, contract_row_pairs, preferred_element_type=jnp.float32
    )
    weight_grad = lax.psum(partial_grad, ("section", "seq"))
    return (decoded[None], weight_grad)


def solution(mesh):
    placed = (
        P("section", "seq"),
        P(None, "chan"),
        P(),
        P(None, None, None, "chan"),
        P("chan", None),
        P("section", "seq", "chan"),
    )
    return jax.shard_map(
        body,
        mesh=mesh,
        in_specs=placed,
        out_specs=(P("section", "seq", "chan"), P("chan", None)),
        check_vma=False,
    )
```

profile of v0, /device:TPU:24, one launch (start us, length us, event | category | flops | bytes accessed | tf_op | source)
XLA Modules:
  0.0 813.8 jit_solution(4729358638135030658)
XLA Ops:
  7.2 0.0 copy-start
  7.2 0.0 copy-start.6
  7.2 0.0 all-gather.4.cloned.1.call-start
  7.2 0.1 eq.26
  7.4 1.1 copy.8
  8.4 0.2 eq.23
  8.6 0.4 eq.24
  9.0 0.0 copy-done
  9.0 1.3 convolution_convert_fusion.1
  10.3 0.0 all-gather.4.cloned.1.call-update
  10.4 0.0 all-gather.6.cloned.1.call-start
  10.4 0.0 copy-done.6
  10.4 0.1 slice_reduce_fusion
  10.5 29.4 %all-gather.4.cloned.1.call-done = bf16[512,1536]{1,0:T(8,128)(2,1)} async-done(((bf16[512,384]{1,0:T(8,128)(2,1)}), bf16[512,1536]{1,0:T(8,128)(2,1)}) %all-gather.4.cloned.1.call-update) | async-done | bytes 1572880 | tf_op jit(solution)/shard_map/all_gather | solution.py:52
  39.8 1.8 fusion
  41.6 2.8 fusion.4
  44.5 3.5 collective-permute-start
  47.9 1.3 collective-permute-start.1
  49.2 2.2 fusion.60
  51.5 0.0 copy-start.1
  51.5 2.0 collective-permute-done.1
  53.4 2.3 fusion.38
  55.7 0.0 collective-permute-done
  55.7 0.0 copy-done.1
  55.7 3.1 fusion.49
  58.8 0.0 all-gather.6.cloned.1.call-update
  58.8 0.0 all-gather.8.cloned.1.call-start
  58.8 28.8 %all-gather.6.cloned.1.call-done = bf16[512,1536]{1,0:T(8,128)(2,1)} async-done(((bf16[512,384]{1,0:T(8,128)(2,1)}), bf16[512,1536]{1,0:T(8,128)(2,1)}) %all-gather.6.cloned.1.call-update) | async-done | bytes 1572880 | tf_op jit(solution)/shard_map/all_gather | solution.py:52
  87.6 1.8 fusion.9
  89.4 2.8 fusion.13
  92.2 1.3 collective-permute-start.3
  93.5 2.2 fusion.56
  95.8 0.0 copy-start.3
  95.8 4.7 collective-permute-start.2
  100.5 0.0 collective-permute-done.3
  100.5 2.3 fusion.34
  102.8 0.0 collective-permute-done.2
  102.8 0.0 copy-done.3
  102.8 3.0 add_convert_fusion.1
  105.8 0.0 all-gather.8.cloned.1.call-update
  105.9 0.0 all-reduce.2.cloned.1.call-start
  105.9 29.4 %all-gather.8.cloned.1.call-done = bf16[512,1536]{1,0:T(8,128)(2,1)} async-done(((bf16[512,384]{1,0:T(8,128)(2,1)}), bf16[512,1536]{1,0:T(8,128)(2,1)}) %all-gather.8.cloned.1.call-update) | async-done | bytes 1572880 | tf_op jit(solution)/shard_map/all_gather | solution.py:52
  135.3 1.8 fusion.18
  137.1 2.8 fusion.22
  139.9 1.5 collective-permute-start.5
  141.4 2.2 fusion.52
  143.7 0.0 copy-start.2
  143.7 4.7 collective-permute-start.4
  148.4 0.0 collective-permute-done.5
  148.4 2.2 fusion.30
  150.6 0.0 copy-start.4
  150.6 0.0 copy-start.5
  150.7 0.0 collective-permute-done.4
  150.7 0.0 copy-done.2
  150.7 2.3 add_convert_fusion
  153.0 0.0 copy-done.4
  153.0 1.2 fusion.74
  154.3 0.0 all-reduce.2.cloned.1.call-update
  154.3 0.0 copy-done.5
  154.3 1.1 fusion.50
  155.4 649.9 %all-reduce.2.cloned.1.call-done = f32[384,384]{1,0:T(8,128)} async-done(((f32[384,384]{1,0:T(8,128)}), f32[384,384]{1,0:T(8,128)}) %all-reduce.2.cloned.1.call-update) | async-done | bytes 589840 | tf_op jit(solution)/shard_map/psum | solution.py:64
  805.3 1.9 copy.10
  (7 shorter events, 0.1 us)
Async XLA Ops:
  7.2 1.8 copy-start
  7.2 3.2 copy-start.6
  7.2 32.7 %all-gather.4.cloned.1.call-start = ((), (), s32[]{:S(2)}) async-start(), calls=%async_computation | async-start | bytes 1966080 | tf_op jit(solution)/shard_map/all_gather | solution.py:52
  10.4 77.3 %all-gather.6.cloned.1.call-start = ((), (), s32[]{:S(2)}) async-start(), calls=%async_computation.1 | async-start | bytes 1966080 | tf_op jit(solution)/shard_map/all_gather | solution.py:52
  44.5 11.2 %collective-permute-start = (bf16[2,1536]{1,0:T(2,128)(2,1)S(1)}, bf16[2,1536]{1,0:T(2,128)(2,1)S(1)}, u32[]{:S(2)}, u32[]{:S(2)}) collective-permute-start(bf16[2,1536]{1,0:T(2,128)(2,1)S(1)} %get-tuple-element.9), channel_id=1, source_target_pairs={{0,4},{4,8},{8,12},{12,16},{16,20},{20,24},{24,28},{28,32},{32,36}... | collective-permute-start | bytes 18440 | tf_op jit(solution)/shard_map/ppermute | solution.py:18
  47.9 5.5 collective-permute-start.1
  51.5 4.2 copy-start.1
  58.8 76.5 %all-gather.8.cloned.1.call-start = ((), (), s32[]{:S(2)}) async-start(), calls=%async_computation.2 | async-start | bytes 1966080 | tf_op jit(solution)/shard_map/all_gather | solution.py:52
  92.2 8.3 %collective-permute-start.3 = (bf16[4,1536]{1,0:T(4,128)(2,1)S(1)}, bf16[4,1536]{1,0:T(4,128)(2,1)S(1)}, u32[]{:S(2)}, u32[]{:S(2)}) collective-permute-start(bf16[4,1536]{1,0:T(4,128)(2,1)S(1)} %get-tuple-element.8), channel_id=1, source_target_pairs={{4,0},{8,4},{12,8},{16,12},{20,16},{24,20},{28,24},{32,28},{36,32}... | collective-permute-start | bytes 36872 | tf_op jit(solution)/shard_map/ppermute | solution.py:19
  95.8 7.0 copy-start.3
  95.8 7.0 collective-permute-start.2
  105.9 699.5 %all-reduce.2.cloned.1.call-start = ((), (), s32[]{:S(2)}) async-start(), calls=%async_computation.3 | async-start | bytes 1179648 | tf_op jit(solution)/shard_map/psum | solution.py:64
  139.9 8.4 %collective-permute-start.5 = (bf16[8,1536]{1,0:T(8,128)(2,1)S(1)}, bf16[8,1536]{1,0:T(8,128)(2,1)S(1)}, u32[]{:S(2)}, u32[]{:S(2)}) collective-permute-start(bf16[8,1536]{1,0:T(8,128)(2,1)S(1)} %get-tuple-element.6), channel_id=1, source_target_pairs={{4,0},{8,4},{12,8},{16,12},{20,16},{24,20},{28,24},{32,28},{36,32}... | collective-permute-start | bytes 73736 | tf_op jit(solution)/shard_map/ppermute | solution.py:19
  143.7 7.0 copy-start.2
  143.7 7.0 collective-permute-start.4
  150.6 2.4 copy-start.4
  150.6 3.6 copy-start.5
Sparse Core Ops, SparseCore 0:
  10.5 29.3 all-gather.3
  58.9 28.6 all-gather.5
  106.0 29.3 all-gather.7
  154.4 650.8 all-reduce.1
where the time goes:
time: 815 us; the launch traced here: 814 us
  waiting for transfers between devices  740 us (91%)
  matrix products  25.6 us (3%)
  starting transfers between devices  17 us (2%)
  between operations  14.1 us (2%)
  other arithmetic  13.7 us (2%)
    psum x1, waiting for transfers between devices, body(): weight_grad = lax.psum(partial_grad, ('section', 'seq'))  650 us
    all_gather x3, waiting for transfers between devices, body(): full_rows = lax.all_gather(stream, 'chan', axis=1, tiled=True)  87.6 us
  transfers between devices with their start and end apart: 10, of which 5 were waited for; matrix products, arithmetic and copies ran while one was open for 2% of the time, Pallas kernels for 0%

commit v1 on v0

--- a/solution.py
+++ b/solution.py
@@ -61,7 +61,8 @@
     partial_grad = lax.dot_general(
         stream, upstream_rows, contract_row_pairs, preferred_element_type=jnp.float32
     )
-    weight_grad = lax.psum(partial_grad, ("section", "seq"))
+    inner = lax.psum(partial_grad, "section")
+    weight_grad = lax.psum(inner, "seq")
     return (decoded[None], weight_grad)
 
 

time: 815 us -> 360 us (0.44)
  waiting for transfers between devices: 740 us -> 285 us
    psum x1 -> x2, waiting for transfers between devices: 650 us -> 196 us  [the longest x1 151 us: body(): weight_grad = lax.psum(inner, 'seq')]
  transfers between devices with their start and end apart: 10 -> 11, of which waited for: 5 -> 6; matrix products, arithmetic and copies ran while one was open for 2% -> 4% of each run, Pallas kernels for 0% -> 0%
where the time goes in v1:
time: 360 us; the launch traced here: 359 us
  waiting for transfers between devices  285 us (79%)
  matrix products  25.6 us (7%)
  starting transfers between devices  17.1 us (5%)
  between operations  14.1 us (4%)
  other arithmetic  13.7 us (4%)
  local copies, waits for them, and re-layouts  3.78 us (1%)
    psum x1, waiting for transfers between devices, body(): weight_grad = lax.psum(inner, 'seq')  151 us
    all_gather x3, waiting for transfers between devices, body(): full_rows = lax.all_gather(stream, 'chan', axis=1, tiled=True)  87.6 us
    psum x1, waiting for transfers between devices, body(): inner = lax.psum(partial_grad, 'section')  44.5 us
    dot_general x6, matrix products, apply_convolution(): jnp.dot(padded[start:start + row_count], kernel_taps[offset], preferred_e...  13.5 us
    ppermute x3, starting transfers between devices, with_halo(): before = lax.ppermute(last, axis, up)  12.8 us
    dot_general x3, matrix products, apply_convolution(): jnp.dot(padded[0:row_count], kernel_taps[0], preferred_element_type=jnp.f...  8.45 us
    convert_element_type x3, other arithmetic, activate(): return jax.nn.gelu(widened * inverse_rms * gain_row).astype(jnp.bfloat16)  8.35 us
  transfers between devices with their start and end apart: 11, of which 6 were waited for; matrix products, arithmetic and copies ran while one was open for 4% of the time, Pallas kernels for 0%

profile of v1, /device:TPU:24, one launch (start us, length us, event | category | flops | bytes accessed | tf_op | source)
XLA Modules:
  0.0 359.5 jit_solution(875136142565981440)
XLA Ops:
  7.2 0.0 copy-start
  7.2 0.0 copy-start.6
  7.2 0.0 all-gather.4.cloned.1.call-start
  7.2 0.1 eq.26
  7.4 1.1 copy.8
  8.4 0.2 eq.23
  8.6 0.4 eq.24
  9.0 0.0 copy-done
  9.0 1.3 convolution_convert_fusion.1
  10.3 0.0 all-gather.4.cloned.1.call-update
  10.4 0.0 all-gather.6.cloned.1.call-start
  10.4 0.0 copy-done.6
  10.4 0.1 slice_reduce_fusion
  10.5 29.4 %all-gather.4.cloned.1.call-done = bf16[512,1536]{1,0:T(8,128)(2,1)} async-done(((bf16[512,384]{1,0:T(8,128)(2,1)}), bf16[512,1536]{1,0:T(8,128)(2,1)}) %all-gather.4.cloned.1.call-update) | async-done | bytes 1572880 | tf_op jit(solution)/shard_map/all_gather | solution.py:52
  39.8 1.8 fusion
  41.6 2.8 fusion.4
  44.5 3.5 collective-permute-start
  47.9 1.3 collective-permute-start.1
  49.2 2.2 fusion.60
  51.5 0.0 copy-start.1
  51.5 2.0 collective-permute-done.1
  53.4 2.3 fusion.38
  55.7 0.0 collective-permute-done
  55.7 0.0 copy-done.1
  55.7 3.1 fusion.49
  58.8 0.0 all-gather.6.cloned.1.call-update
  58.8 0.0 all-gather.8.cloned.1.call-start
  58.8 28.8 %all-gather.6.cloned.1.call-done = bf16[512,1536]{1,0:T(8,128)(2,1)} async-done(((bf16[512,384]{1,0:T(8,128)(2,1)}), bf16[512,1536]{1,0:T(8,128)(2,1)}) %all-gather.6.cloned.1.call-update) | async-done | bytes 1572880 | tf_op jit(solution)/shard_map/all_gather | solution.py:52
  87.6 1.8 fusion.9
  89.4 2.8 fusion.13
  92.2 1.3 collective-permute-start.3
  93.5 2.2 fusion.56
  95.8 0.0 copy-start.3
  95.8 4.7 %collective-permute-start.2 = (bf16[4,1536]{1,0:T(4,128)(2,1)S(1)}, bf16[4,1536]{1,0:T(4,128)(2,1)S(1)}, u32[]{:S(2)}, u32[]{:S(2)}) collective-permute-start(bf16[4,1536]{1,0:T(4,128)(2,1)S(1)} %get-tuple-element.7), channel_id=1, source_target_pairs={{0,4},{4,8},{8,12},{12,16},{16,20},{20,24},{24,28},{28,32},{32,36}... | collective-permute-start | bytes 36872 | tf_op jit(solution)/shard_map/ppermute | solution.py:18
  100.5 0.0 collective-permute-done.3
  100.5 2.3 fusion.34
  102.8 0.0 collective-permute-done.2
  102.8 0.0 copy-done.3
  102.8 3.0 add_convert_fusion.1
  105.8 0.0 all-gather.8.cloned.1.call-update
  105.9 0.0 all-reduce.3.cloned.1.call-start
  105.9 29.4 %all-gather.8.cloned.1.call-done = bf16[512,1536]{1,0:T(8,128)(2,1)} async-done(((bf16[512,384]{1,0:T(8,128)(2,1)}), bf16[512,1536]{1,0:T(8,128)(2,1)}) %all-gather.8.cloned.1.call-update) | async-done | bytes 1572880 | tf_op jit(solution)/shard_map/all_gather | solution.py:52
  135.3 1.8 fusion.18
  137.1 2.8 fusion.22
  139.9 1.5 collective-permute-start.5
  141.4 2.2 fusion.52
  143.7 0.0 copy-start.2
  143.7 4.7 %collective-permute-start.4 = (bf16[8,1536]{1,0:T(8,128)(2,1)S(1)}, bf16[8,1536]{1,0:T(8,128)(2,1)S(1)}, u32[]{:S(2)}, u32[]{:S(2)}) collective-permute-start(bf16[8,1536]{1,0:T(8,128)(2,1)S(1)} %get-tuple-element.5), channel_id=1, source_target_pairs={{0,4},{4,8},{8,12},{12,16},{16,20},{20,24},{24,28},{28,32},{32,36}... | collective-permute-start | bytes 73736 | tf_op jit(solution)/shard_map/ppermute | solution.py:18
  148.4 0.0 collective-permute-done.5
  148.4 2.2 fusion.30
  150.6 0.0 copy-start.4
  150.6 0.0 copy-start.5
  150.7 0.0 collective-permute-done.4
  150.7 0.0 copy-done.2
  150.7 2.3 add_convert_fusion
  153.0 0.0 copy-done.4
  153.0 1.2 fusion.74
  154.3 0.0 all-reduce.3.cloned.1.call-update
  154.3 0.0 all-reduce.5.cloned.1.call-start
  154.3 44.5 %all-reduce.3.cloned.1.call-done = f32[384,384]{1,0:T(8,128)} async-done(((f32[384,384]{1,0:T(8,128)}), f32[384,384]{1,0:T(8,128)}) %all-reduce.3.cloned.1.call-update) | async-done | bytes 589840 | tf_op jit(solution)/shard_map/psum | solution.py:64
  198.8 0.0 all-reduce.5.cloned.1.call-update
  198.9 1.1 fusion.50
  200.0 151.0 %all-reduce.5.cloned.1.call-done = f32[384,384]{1,0:T(8,128)} async-done(((f32[384,384]{1,0:T(8,128)}), f32[384,384]{1,0:T(8,128)}) %all-reduce.5.cloned.1.call-update) | async-done | bytes 589840 | tf_op jit(solution)/shard_map/psum | solution.py:65
  351.0 1.9 copy.11
  (8 shorter events, 0.1 us)
Async XLA Ops:
  7.2 1.8 copy-start
  7.2 3.2 copy-start.6
  7.2 32.7 %all-gather.4.cloned.1.call-start = ((), (), s32[]{:S(2)}) async-start(), calls=%async_computation | async-start | bytes 1966080 | tf_op jit(solution)/shard_map/all_gather | solution.py:52
  10.4 77.3 %all-gather.6.cloned.1.call-start = ((), (), s32[]{:S(2)}) async-start(), calls=%async_computation.1 | async-start | bytes 1966080 | tf_op jit(solution)/shard_map/all_gather | solution.py:52
  44.5 11.2 %collective-permute-start = (bf16[2,1536]{1,0:T(2,128)(2,1)S(1)}, bf16[2,1536]{1,0:T(2,128)(2,1)S(1)}, u32[]{:S(2)}, u32[]{:S(2)}) collective-permute-start(bf16[2,1536]{1,0:T(2,128)(2,1)S(1)} %get-tuple-element.9), channel_id=1, source_target_pairs={{0,4},{4,8},{8,12},{12,16},{16,20},{20,24},{24,28},{28,32},{32,36}... | collective-permute-start | bytes 18440 | tf_op jit(solution)/shard_map/ppermute | solution.py:18
  47.9 5.5 %collective-permute-start.1 = (bf16[2,1536]{1,0:T(2,128)(2,1)S(1)}, bf16[2,1536]{1,0:T(2,128)(2,1)S(1)}, u32[]{:S(2)}, u32[]{:S(2)}) collective-permute-start(bf16[2,1536]{1,0:T(2,128)(2,1)S(1)} %get-tuple-element.10), channel_id=1, source_target_pairs={{4,0},{8,4},{12,8},{16,12},{20,16},{24,20},{28,24},{32,28},{36,32}... | collective-permute-start | bytes 18440 | tf_op jit(solution)/shard_map/ppermute | solution.py:19
  51.5 4.2 %copy-start.1 = (bf16[512,384]{1,0:T(8,128)(2,1)S(1)}, bf16[512,384]{1,0:T(8,128)(2,1)}, u32[]{:S(2)}) copy-start(bf16[512,384]{1,0:T(8,128)(2,1)} %convolution_convert_fusion.1) | copy-start | bytes 1179652
  58.8 76.5 %all-gather.8.cloned.1.call-start = ((), (), s32[]{:S(2)}) async-start(), calls=%async_computation.2 | async-start | bytes 1966080 | tf_op jit(solution)/shard_map/all_gather | solution.py:52
  92.2 8.3 %collective-permute-start.3 = (bf16[4,1536]{1,0:T(4,128)(2,1)S(1)}, bf16[4,1536]{1,0:T(4,128)(2,1)S(1)}, u32[]{:S(2)}, u32[]{:S(2)}) collective-permute-start(bf16[4,1536]{1,0:T(4,128)(2,1)S(1)} %get-tuple-element.8), channel_id=1, source_target_pairs={{4,0},{8,4},{12,8},{16,12},{20,16},{24,20},{28,24},{32,28},{36,32}... | collective-permute-start | bytes 36872 | tf_op jit(solution)/shard_map/ppermute | solution.py:19
  95.8 7.0 %copy-start.3 = (bf16[512,384]{1,0:T(8,128)(2,1)S(1)}, bf16[512,384]{1,0:T(8,128)(2,1)}, u32[]{:S(2)}) copy-start(bf16[512,384]{1,0:T(8,128)(2,1)} %fusion.49) | copy-start | bytes 1179652
  95.8 7.0 %collective-permute-start.2 = (bf16[4,1536]{1,0:T(4,128)(2,1)S(1)}, bf16[4,1536]{1,0:T(4,128)(2,1)S(1)}, u32[]{:S(2)}, u32[]{:S(2)}) collective-permute-start(bf16[4,1536]{1,0:T(4,128)(2,1)S(1)} %get-tuple-element.7), channel_id=1, source_target_pairs={{0,4},{4,8},{8,12},{12,16},{16,20},{20,24},{24,28},{28,32},{32,36}... | collective-permute-start | bytes 36872 | tf_op jit(solution)/shard_map/ppermute | solution.py:18
  105.9 93.0 %all-reduce.3.cloned.1.call-start = ((), (), s32[]{:S(2)}) async-start(), calls=%async_computation.3 | async-start | bytes 1179648 | tf_op jit(solution)/shard_map/psum | solution.py:64
  139.9 8.4 %collective-permute-start.5 = (bf16[8,1536]{1,0:T(8,128)(2,1)S(1)}, bf16[8,1536]{1,0:T(8,128)(2,1)S(1)}, u32[]{:S(2)}, u32[]{:S(2)}) collective-permute-start(bf16[8,1536]{1,0:T(8,128)(2,1)S(1)} %get-tuple-element.6), channel_id=1, source_target_pairs={{4,0},{8,4},{12,8},{16,12},{20,16},{24,20},{28,24},{32,28},{36,32}... | collective-permute-start | bytes 73736 | tf_op jit(solution)/shard_map/ppermute | solution.py:19
  143.7 7.0 %copy-start.2 = (bf16[512,384]{1,0:T(8,128)(2,1)S(1)}, bf16[512,384]{1,0:T(8,128)(2,1)}, u32[]{:S(2)}) copy-start(bf16[512,384]{1,0:T(8,128)(2,1)} %add_convert_fusion.1) | copy-start | bytes 1179652
  143.7 7.0 %collective-permute-start.4 = (bf16[8,1536]{1,0:T(8,128)(2,1)S(1)}, bf16[8,1536]{1,0:T(8,128)(2,1)S(1)}, u32[]{:S(2)}, u32[]{:S(2)}) collective-permute-start(bf16[8,1536]{1,0:T(8,128)(2,1)S(1)} %get-tuple-element.5), channel_id=1, source_target_pairs={{0,4},{4,8},{8,12},{12,16},{16,20},{20,24},{24,28},{28,32},{32,36}... | collective-permute-start | bytes 73736 | tf_op jit(solution)/shard_map/ppermute | solution.py:18
  150.6 2.4 copy-start.4
  150.6 48.2 %copy-start.5 = (bf16[384,384]{1,0:T(8,128)(2,1)S(1)}, bf16[384,384]{1,0:T(8,128)(2,1)}, u32[]{:S(2)}) copy-start(bf16[384,384]{1,0:T(8,128)(2,1)} %param.10) | copy-start | bytes 884740
  154.3 196.7 %all-reduce.5.cloned.1.call-start = ((), (), s32[]{:S(2)}) async-start(), calls=%async_computation.4 | async-start | bytes 1179648 | tf_op jit(solution)/shard_map/psum | solution.py:65
Sparse Core Ops, SparseCore 0:
  10.5 29.3 all-gather.3
  58.9 28.6 all-gather.5
  106.0 29.3 all-gather.7
  154.4 44.3 all-reduce.2
  202.4 148.5 all-reduce.4
